TPU v7x, 32 devices: a whole 2x2x4 slice. The times are simulated.
32 devices in a mesh: seq: 8 (over z, y), head: 4 (over x, core).
Axes of the slice: x: 2, y: 2, z: 4, core: 2. Of those that a mesh axis runs over, the one named last changes fastest.
Arguments:
- layer_input: bfloat16 [4096, 768], P('seq', 'head'), may hold values from -6 to 6
- ln1_gain: float32 [768], replicated, may hold values from 0.5 to 1.5
- ln1_bias: float32 [768], replicated, may hold values from -3 to 3
- w_query: bfloat16 [768, 768], P(None, 'head'), may hold values from -0.21875 to 0.21875
- b_query: float32 [768], P('head'), may hold values from -3 to 3
- w_key: bfloat16 [768, 768], P(None, 'head'), may hold values from -0.3125 to 0.3125
- w_value: bfloat16 [768, 768], P(None, 'head'), may hold values from -0.21875 to 0.21875
- b_value: float32 [768], P('head'), may hold values from -1.2 to 1.2
- sub_gain: float32 [768], P('head'), may hold values from 0.5 to 1.5
- sub_bias: float32 [768], P('head'), may hold values from -3 to 3
- w_out: bfloat16 [768, 768], P('head'), may hold values from -0.21875 to 0.21875
- b_out: float32 [768], replicated, may hold values from -3 to 3
- ln2_gain: float32 [768], replicated, may hold values from 0.5 to 1.5
- ln2_bias: float32 [768], replicated, may hold values from -3 to 3
- w_up: bfloat16 [768, 3072], P(None, 'head'), may hold values from -0.21875 to 0.21875
- b_up: float32 [3072], P('head'), may hold values from -3 to 3
- w_down: bfloat16 [3072, 768], P('head'), may hold values from -0.109375 to 0.109375
- b_down: float32 [768], replicated, may hold values from -3 to 3
- cotangent: bfloat16 [4096, 768], P('seq', 'head'), may hold values from -6 to 6
- row_lengths: int32 [6], replicated, may hold values from 1 to 3072, 4096 in all
Outputs:
- layer_output: bfloat16 [4096, 768], P('seq', 'head')
- grad_input: float32 [4096, 768], P('seq', 'head')
- grad_ln1_gain: float32 [768], replicated
- grad_ln1_bias: float32 [768], replicated
- grad_w_query: float32 [768, 768], P(None, 'head')
- grad_b_query: float32 [768], P('head')
- grad_w_key: float32 [768, 768], P(None, 'head')
- grad_w_value: float32 [768, 768], P(None, 'head')
- grad_b_value: float32 [768], P('head')
- grad_sub_gain: float32 [768], P('head')
- grad_sub_bias: float32 [768], P('head')
- grad_w_out: float32 [768, 768], P('head')
- grad_b_out: float32 [768], replicated
- grad_ln2_gain: float32 [768], replicated
- grad_ln2_bias: float32 [768], replicated
- grad_w_up: float32 [768, 3072], P(None, 'head')
- grad_b_up: float32 [3072], P('head')
- grad_w_down: float32 [3072, 768], P('head')
- grad_b_down: float32 [768], replicated
Inputs may be any that keep to these rules, and one draw needn't show every extreme that they name: `row_lengths`: the 6 row lengths sum to 4096, and the longest is exactly 3072.
All inputs are finite; a program needn't handle non-finite values.
Results may differ from a plain program's by a relative error of at most 0.018.
Values may be sent and summed in bfloat16 or wider, within the bound.
No kernel may reach another device: no remote copies, remote signals or barrier semaphores. Data moves between devices by JAX's collectives and lax.ppermute only.
A program may use at most 256 MiB of HBM per device.

v0:
```python
import math
import jax
import jax.numpy as jnp
from jax import lax
from jax.sharding import PartitionSpec as P

HEAD_DIM = 64
SEG = 2048
eps = 1e-05
segment_scales = (1, 2, 4, 8, 16)
dilation_steps = (1, 2, 4, 6, 12)


def layer_norm(inputs, norm_gain, norm_bias):
    center = inputs - jnp.mean(inputs, axis=-1, keepdims=True)
    spread = jnp.mean(center * center, axis=-1, keepdims=True)
    return center * lax.rsqrt(spread + eps) * norm_gain + norm_bias


def token_places(positions, lengths):
    row_ends = jnp.cumsum(lengths)
    starts = row_ends - lengths
    row_of = jnp.sum((positions[:, None] >= row_ends[None, :]).astype(jnp.int32), axis=1)
    onehot = (row_of[:, None] == jnp.arange(lengths.shape[0], dtype=jnp.int32)[None, :]).astype(
        jnp.int32
    )
    row_place = positions - jnp.sum(onehot * starts[None, :], axis=1)
    return (row_of, row_place)


def pattern_count(head_ids, query_row, query_place, key_row, key_place):
    allowed = (query_row[:, None] == key_row[None, :]) & (
        key_place[None, :] <= query_place[:, None]
    )
    counted = jnp.zeros((head_ids.shape[0], query_row.shape[0], key_row.shape[0]), jnp.float32)
    for scale_factor, step_size in zip(segment_scales, dilation_steps):
        seg_width = SEG * scale_factor
        same_seg = allowed & (query_place[:, None] // seg_width == key_place[None, :] // seg_width)
        offset = head_ids % step_size
        query_on = (query_place % seg_width % step_size)[None, :] == offset[:, None]
        key_on = (key_place % seg_width % step_size)[None, :] == offset[:, None]
        counted = counted + (same_seg[None] & query_on[:, :, None] & key_on[:, None, :]).astype(
            jnp.float32
        )
    return counted


def fold_keys(running, pieces, queries, head_ids, query_row, query_place, lengths, score_scale):
    key_rows, values = pieces
    piece_rows = key_rows.shape[0]
    block_rows = math.gcd(piece_rows, 2048)
    local_heads = queries.shape[0]
    key_blocks = key_rows.reshape(piece_rows // block_rows, block_rows, local_heads, -1)
    value_blocks = values.reshape(piece_rows // block_rows, block_rows, local_heads, -1)
    offsets = jnp.arange(piece_rows // block_rows, dtype=jnp.int32) * block_rows

    def advance(status, element):
        highest, totals, running_sum = status
        key_blk, value_blk, block_first = element
        key_row, key_place = token_places(
            block_first + jnp.arange(block_rows, dtype=jnp.int32), lengths
        )
        counted = pattern_count(head_ids, query_row, query_place, key_row, key_place)
        scores = (
            jnp.einsum("hqd,khd->hqk", queries, key_blk, preferred_element_type=jnp.float32)
            * score_scale
        )
        masked = jnp.where(counted > 0, scores, -1e30)
        new_high = jnp.maximum(highest, jnp.max(masked, axis=-1))
        weights = counted * jnp.exp(masked - new_high[..., None])
        factor = jnp.exp(highest - new_high)
        totals = totals * factor + jnp.sum(weights, axis=-1)
        running_sum = running_sum * factor[..., None] + jnp.einsum(
            "hqk,khd->hqd",
            weights.astype(jnp.bfloat16),
            value_blk,
            preferred_element_type=jnp.float32,
        )
        return ((new_high, totals, running_sum), None)

    running, unused = lax.scan(advance, running, (key_blocks, value_blocks, offsets))
    return running


def shards(
    layer_input,
    ln1_gain,
    ln1_bias,
    w_query,
    b_query,
    w_key,
    w_value,
    b_value,
    sub_gain,
    sub_bias,
    w_out,
    b_out,
    ln2_gain,
    ln2_bias,
    w_up,
    b_up,
    w_down,
    b_down,
    cotangent,
    row_lengths,
):
    rows_local = layer_input.shape[0]
    slice_width = layer_input.shape[1]
    head_share = w_query.shape[1]
    local_heads = head_share // HEAD_DIM
    head_pos = lax.axis_index("head")
    seq_pos = lax.axis_index("seq")
    full_width = head_share * lax.axis_size("head")
    score_scale = HEAD_DIM ** (-0.5)
    head_ids = head_pos * local_heads + jnp.arange(local_heads, dtype=jnp.int32)
    own_index = seq_pos * rows_local + jnp.arange(rows_local, dtype=jnp.int32)
    query_row, query_place = token_places(own_index, row_lengths)
    input_whole = lax.all_gather(layer_input, "head", axis=1, tiled=True).astype(jnp.float32)
    normed = layer_norm(input_whole, ln1_gain, ln1_bias).astype(jnp.bfloat16)
    queries = (jnp.dot(normed, w_query, preferred_element_type=jnp.float32) + b_query).astype(
        jnp.bfloat16
    )
    key_rows = jnp.dot(normed, w_key, preferred_element_type=jnp.float32).astype(jnp.bfloat16)
    values = (jnp.dot(normed, w_value, preferred_element_type=jnp.float32) + b_value).astype(
        jnp.bfloat16
    )
    query_heads = queries.reshape(rows_local, local_heads, HEAD_DIM).transpose(1, 0, 2)
    start_state = (
        jnp.full((local_heads, rows_local), -1e30, jnp.float32),
        jnp.zeros((local_heads, rows_local), jnp.float32),
        jnp.zeros((local_heads, rows_local, HEAD_DIM), jnp.float32),
    )
    highest, totals, running_sum = fold_keys(
        start_state,
        (
            lax.all_gather(key_rows, "seq", axis=0, tiled=True),
            lax.all_gather(values, "seq", axis=0, tiled=True),
        ),
        query_heads,
        head_ids,
        query_row,
        query_place,
        row_lengths,
        score_scale,
    )
    attended = running_sum / totals[..., None]
    log_total = highest + jnp.log(totals)
    mixed_heads = attended.transpose(1, 0, 2).reshape(rows_local, head_share)
    row_sum, row_square = lax.psum(
        (jnp.sum(mixed_heads, axis=1), jnp.sum(mixed_heads * mixed_heads, axis=1)), "head"
    )
    mean_value = row_sum / full_width
    inv_std = lax.rsqrt(row_square / full_width - mean_value * mean_value + eps)
    centered = (mixed_heads - mean_value[:, None]) * inv_std[:, None]
    sub_out = (centered * sub_gain + sub_bias).astype(jnp.bfloat16)
    projected = lax.psum_scatter(
        jnp.dot(sub_out, w_out, preferred_element_type=jnp.float32).astype(jnp.bfloat16),
        "head",
        scatter_dimension=1,
        tiled=True,
    ).astype(jnp.float32)
    out_bias_share = lax.dynamic_slice_in_dim(b_out, head_pos * slice_width, slice_width, 0)
    middle = layer_input.astype(jnp.float32) + (projected + out_bias_share)
    middle_whole = lax.all_gather(middle.astype(jnp.bfloat16), "head", axis=1, tiled=True).astype(
        middle.dtype
    )
    normed_mid = layer_norm(middle_whole, ln2_gain, ln2_bias).astype(jnp.bfloat16)
    inner_act = jnp.dot(normed_mid, w_up, preferred_element_type=jnp.float32) + b_up
    active = jax.nn.gelu(inner_act, approximate=False).astype(jnp.bfloat16)
    ffn_out = lax.psum_scatter(
        jnp.dot(active, w_down, preferred_element_type=jnp.float32).astype(jnp.bfloat16),
        "head",
        scatter_dimension=1,
        tiled=True,
    ).astype(jnp.float32)
    down_bias_share = lax.dynamic_slice_in_dim(b_down, head_pos * slice_width, slice_width, 0)
    layer_output = (middle + (ffn_out + down_bias_share)).astype(jnp.bfloat16)
    grad_whole = lax.all_gather(cotangent, "head", axis=1, tiled=True)
    grad_float = grad_whole.astype(jnp.float32)
    grad_w_down = jnp.dot(active.T, grad_whole, preferred_element_type=jnp.float32)
    grad_b_down = jnp.sum(grad_float, axis=0)
    grad_active = jnp.dot(grad_whole, w_down.T, preferred_element_type=jnp.float32)
    unused, gelu_back = jax.vjp(lambda inputs: jax.nn.gelu(inputs, approximate=False), inner_act)
    grad_inner = gelu_back(grad_active)[0].astype(jnp.bfloat16)
    grad_w_up = jnp.dot(normed_mid.T, grad_inner, preferred_element_type=jnp.float32)
    grad_b_up = jnp.sum(grad_inner.astype(jnp.float32), axis=0)
    grad_norm_mid = lax.psum(
        jnp.dot(grad_inner, w_up.T, preferred_element_type=jnp.float32).astype(jnp.bfloat16), "head"
    ).astype(jnp.float32)
    unused, mid_back = jax.vjp(layer_norm, middle_whole, ln2_gain, ln2_bias)
    grad_mid_norm, grad_ln2_gain, grad_ln2_bias = mid_back(grad_norm_mid)
    grad_middle = grad_float + grad_mid_norm
    grad_branch = grad_middle.astype(jnp.bfloat16)
    grad_b_out = jnp.sum(grad_branch.astype(jnp.float32), axis=0)
    grad_w_out = jnp.dot(sub_out.T, grad_branch, preferred_element_type=jnp.float32)
    grad_sub = jnp.dot(grad_branch, w_out.T, preferred_element_type=jnp.float32)
    grad_sub_gain = jnp.sum(grad_sub * centered, axis=0)
    grad_sub_bias = jnp.sum(grad_sub, axis=0)
    grad_hat = grad_sub * sub_gain
    hat_sum, hat_cross = lax.psum(
        (jnp.sum(grad_hat, axis=1), jnp.sum(grad_hat * centered, axis=1)), "head"
    )
    grad_mixed = inv_std[:, None] * (
        grad_hat - hat_sum[:, None] / full_width - centered * hat_cross[:, None] / full_width
    )
    grad_heads = (
        grad_mixed.reshape(rows_local, local_heads, HEAD_DIM)
        .transpose(1, 0, 2)
        .astype(jnp.bfloat16)
    )
    dot_term = jnp.sum(grad_heads.astype(jnp.float32) * attended, axis=-1)
    key_all, value_all = (
        lax.all_gather(key_rows, "seq", axis=0, tiled=True),
        lax.all_gather(values, "seq", axis=0, tiled=True),
    )
    total_rows = key_all.shape[0]
    block_rows = math.gcd(total_rows, 2048)
    key_blocks = key_all.reshape(total_rows // block_rows, block_rows, local_heads, HEAD_DIM)
    value_blocks = value_all.reshape(total_rows // block_rows, block_rows, local_heads, HEAD_DIM)
    offsets = jnp.arange(total_rows // block_rows, dtype=jnp.int32) * block_rows

    def score_parts(
        query_blk, grad_blk, log_blk, dot_blk, q_row, q_place, key_blk, value_blk, k_row, k_place
    ):
        counted = pattern_count(head_ids, q_row, q_place, k_row, k_place)
        scores = (
            jnp.einsum("hqd,khd->hqk", query_blk, key_blk, preferred_element_type=jnp.float32)
            * score_scale
        )
        masked = jnp.where(counted > 0, scores, -1e30)
        weights_norm = counted * jnp.exp(masked - log_blk[..., None])
        grad_probs = jnp.einsum(
            "hqd,khd->hqk", grad_blk, value_blk, preferred_element_type=jnp.float32
        )
        grad_scores = (weights_norm * (grad_probs - dot_blk[..., None])).astype(jnp.bfloat16)
        return (weights_norm, grad_scores)

    def back_step(grad_query_sum, element):
        key_blk, value_blk, block_first = element
        key_row, key_place = token_places(
            block_first + jnp.arange(block_rows, dtype=jnp.int32), row_lengths
        )
        weights_norm, grad_scores = score_parts(
            query_heads,
            grad_heads,
            log_total,
            dot_term,
            query_row,
            query_place,
            key_blk,
            value_blk,
            key_row,
            key_place,
        )
        grad_query_sum = grad_query_sum + jnp.einsum(
            "hqk,khd->hqd", grad_scores, key_blk, preferred_element_type=jnp.float32
        )
        grad_value = jnp.einsum(
            "hqk,hqd->khd",
            weights_norm.astype(jnp.bfloat16),
            grad_heads,
            preferred_element_type=jnp.float32,
        )
        grad_key = jnp.einsum(
            "hqk,hqd->khd", grad_scores, query_heads, preferred_element_type=jnp.float32
        )
        key_terms = jnp.concatenate(
            [grad_key.reshape(block_rows, -1) * score_scale, grad_value.reshape(block_rows, -1)],
            axis=1,
        )
        return (grad_query_sum, key_terms)

    query_zero = jnp.zeros((local_heads, rows_local, HEAD_DIM), jnp.float32)
    grad_query_sum, key_terms = lax.scan(back_step, query_zero, (key_blocks, value_blocks, offsets))
    key_terms = key_terms.reshape(total_rows, 2 * head_share)
    kv_grads = lax.psum_scatter(key_terms, "seq", scatter_dimension=0, tiled=True)
    grad_keys = kv_grads[:, :head_share].astype(jnp.bfloat16)
    grad_values = kv_grads[:, head_share:].astype(jnp.bfloat16)
    grad_queries = (grad_query_sum * score_scale).transpose(1, 0, 2).reshape(rows_local, head_share)
    grad_queries = grad_queries.astype(jnp.bfloat16)
    grad_w_query = jnp.dot(normed.T, grad_queries, preferred_element_type=jnp.float32)
    grad_b_query = jnp.sum(grad_queries.astype(jnp.float32), axis=0)
    grad_w_key = jnp.dot(normed.T, grad_keys, preferred_element_type=jnp.float32)
    grad_w_value = jnp.dot(normed.T, grad_values, preferred_element_type=jnp.float32)
    grad_b_value = jnp.sum(grad_values.astype(jnp.float32), axis=0)
    grad_normed = (
        jnp.dot(grad_queries, w_query.T, preferred_element_type=jnp.float32)
        + jnp.dot(grad_keys, w_key.T, preferred_element_type=jnp.float32)
        + jnp.dot(grad_values, w_value.T, preferred_element_type=jnp.float32)
    )
    grad_normed = lax.psum(grad_normed.astype(jnp.bfloat16), "head").astype(jnp.float32)
    unused, input_back = jax.vjp(layer_norm, input_whole, ln1_gain, ln1_bias)
    grad_in_norm, grad_ln1_gain, grad_ln1_bias = input_back(grad_normed)
    grad_input_whole = grad_middle + grad_in_norm
    grad_input = lax.dynamic_slice_in_dim(grad_input_whole, head_pos * slice_width, slice_width, 1)
    summed = lax.psum(
        (
            grad_ln1_gain,
            grad_ln1_bias,
            grad_w_query,
            grad_b_query,
            grad_w_key,
            grad_w_value,
            grad_b_value,
            grad_sub_gain,
            grad_sub_bias,
            grad_w_out,
            grad_b_out,
            grad_ln2_gain,
            grad_ln2_bias,
            grad_w_up,
            grad_b_up,
            grad_w_down,
            grad_b_down,
        ),
        "seq",
    )
    return (layer_output, grad_input) + tuple(summed)


def solution(mesh):
    in_specs = (
        P("seq", "head"),
        P(),
        P(),
        P(None, "head"),
        P("head"),
        P(None, "head"),
        P(None, "head"),
        P("head"),
        P("head"),
        P("head"),
        P("head", None),
        P(),
        P(),
        P(),
        P(None, "head"),
        P("head"),
        P("head", None),
        P(),
        P("seq", "head"),
        P(),
    )
    out_specs = (
        P("seq", "head"),
        P("seq", "head"),
        P(),
        P(),
        P(None, "head"),
        P("head"),
        P(None, "head"),
        P(None, "head"),
        P("head"),
        P("head"),
        P("head"),
        P("head", None),
        P(),
        P(),
        P(),
        P(None, "head"),
        P("head"),
        P("head", None),
        P(),
    )
    return jax.shard_map(shards, mesh=mesh, in_specs=in_specs, out_specs=out_specs, check_vma=False)
```

profile of v0, /device:TPU:0, one launch (start us, length us, event | category | flops | bytes accessed | tf_op | source)
XLA Modules:
  0.0 842.9 jit_solution(17732856070422200237)
XLA Ops:
  7.3 10.4 %all_gather.17 = bf16[512,768]{0,1:T(8,128)(2,1)S(1)} all-gather(bf16[512,192]{0,1:T(8,128)(2,1)} %param.24), channel_id=1, replica_groups=mesh['seq'=8,'head'=4] {'head'}, dimensions={1}, use_global_device_ids=true | all-gather | bytes 983040 | tf_op jit(solution)/shard_map/all_gather | solution.py:118
  22.7 43.9 %all-gather.3.cloned.1.call-done = bf16[4096,192]{0,1:T(8,128)(2,1)} async-done(((bf16[512,192]{0,1:T(8,128)(2,1)}), bf16[4096,192]{0,1:T(8,128)(2,1)}) %all-gather.3.cloned.1.call-update) | async-done | bytes 1572880 | tf_op jit(solution)/shard_map/all_gather | solution.py:136
  66.6 2.9 reshape.2798
  69.5 1.8 copy.68
  71.2 41.5 %all-gather.5.cloned.1.call-done = bf16[4096,192]{0,1:T(8,128)(2,1)} async-done(((bf16[512,192]{0,1:T(8,128)(2,1)}), bf16[4096,192]{0,1:T(8,128)(2,1)}) %all-gather.5.cloned.1.call-update) | async-done | bytes 1572880 | tf_op jit(solution)/shard_map/all_gather | solution.py:137
  112.8 2.9 reshape.2800
  115.6 1.8 copy.69
  117.4 77.7 %while.42 = (s32[]{:T(128)}, f32[3,512]{1,0:T(4,128)S(1)}, f32[3,512]{1,0:T(4,128)}, f32[3,512,64]{1,2,0:T(8,128)}, s32[512]{0:T(512)S(1)}, /*index=5*/s32[2]{0:...) while((s32[]{:T(128)}, f32[3,512]{1,0:T(4,128)S(1)}, ...), condition=%wide.region_10.11_spmd.clone.clone.clone, body=%wide.region_5.10_spmd.clone.clone.clone.sunk | while | flops 955956864 | bytes 106965376 | solution.py:81
  120.3 4.1 compare_and_fusion.12
  125.2 12.1 %fusion.202 = (f32[3,512]{1,0:T(4,128)S(1)}, f32[3,2048,512]{2,1,0:T(8,128)}) fusion(f32[512,2048]{0,1:T(8,128)S(1)} %get-tuple-element.1711, pred[3,2048]{1,0:T(4,128)(4,1)S(1)} %broadcast_compare_fusion.38, pred[3,512]{1,0:T(4,128)(4,1)S(1)} %broadcast_compare_fusion.39, pred[512,2048]{0,1:T(8,128)(4,1)S(1)} %get-tuple-element.1716, ...), kind=kOutput, calls=%fused_computation.7.clone.1 | convolution fusion | flops 465566208 | bytes 22001668 | tf_op jit(solution)/shard_map/while/body/eval_jaxpr/hqd,khd->hqk/dot_general | solution.py:65
  137.4 16.7 %fusion.203 = (f32[3,512]{1,0:T(4,128)S(1)}, bf16[3,512,2048]{1,2,0:T(8,128)(2,1)S(1)}) fusion(f32[3,512]{1,0:T(4,128)S(1)} %select_maximum_fusion.2, f32[3,2048,512]{2,1,0:T(8,128)} %get-tuple-element.1730, pred[3,2048]{1,0:T(4,128)(4,1)S(1)} %broadcast_compare_fusion.38, pred[3,512]{1,0:T(4,128)(4,1)S(1)} %broadcast_compare_fusion.39, ...), kind=kLoop, calls=%fused_computation.388.clone.1 | loop fusion | flops 72350208 | bytes 27305984 | tf_op jit(solution)/shard_map/while/body/eval_jaxpr/reduce_sum | solution.py:72
  159.2 4.1 compare_and_fusion.12
  164.1 12.1 %fusion.202 = (f32[3,512]{1,0:T(4,128)S(1)}, f32[3,2048,512]{2,1,0:T(8,128)}) fusion(f32[512,2048]{0,1:T(8,128)S(1)} %get-tuple-element.1711, pred[3,2048]{1,0:T(4,128)(4,1)S(1)} %broadcast_compare_fusion.38, pred[3,512]{1,0:T(4,128)(4,1)S(1)} %broadcast_compare_fusion.39, pred[512,2048]{0,1:T(8,128)(4,1)S(1)} %get-tuple-element.1716, ...), kind=kOutput, calls=%fused_computation.7.clone.1 | convolution fusion | flops 465566208 | bytes 22001668 | tf_op jit(solution)/shard_map/while/body/eval_jaxpr/hqd,khd->hqk/dot_general | solution.py:65
  176.3 16.7 %fusion.203 = (f32[3,512]{1,0:T(4,128)S(1)}, bf16[3,512,2048]{1,2,0:T(8,128)(2,1)S(1)}) fusion(f32[3,512]{1,0:T(4,128)S(1)} %select_maximum_fusion.2, f32[3,2048,512]{2,1,0:T(8,128)} %get-tuple-element.1730, pred[3,2048]{1,0:T(4,128)(4,1)S(1)} %broadcast_compare_fusion.38, pred[3,512]{1,0:T(4,128)(4,1)S(1)} %broadcast_compare_fusion.39, ...), kind=kLoop, calls=%fused_computation.388.clone.1 | loop fusion | flops 72350208 | bytes 27305984 | tf_op jit(solution)/shard_map/while/body/eval_jaxpr/reduce_sum | solution.py:72
  196.4 6.0 all-reduce.3
  204.9 8.7 %all_gather.21 = bf16[512,768]{0,1:T(8,128)(2,1)S(1)} all-gather(bf16[512,192]{0,1:T(8,128)(2,1)} %param.42), channel_id=1, replica_groups=mesh['seq'=8,'head'=4] {'head'}, dimensions={1}, use_global_device_ids=true | all-gather | bytes 983040 | tf_op jit(solution)/shard_map/all_gather | solution.py:178
  213.6 11.9 %reduce-scatter.4.cloned.1.call-done = bf16[512,192]{0,1:T(8,128)(2,1)} async-done(((bf16[512,768]{0,1:T(8,128)(2,1)}), bf16[512,192]{0,1:T(8,128)(2,1)}) %reduce-scatter.4.cloned.1.call-update) | async-done | bytes 196624 | tf_op jit(solution)/shard_map/reduce_scatter | solution.py:156
  226.7 8.7 %all_gather.20 = bf16[512,768]{0,1:T(8,128)(2,1)S(1)} all-gather(bf16[512,192]{0,1:T(8,128)(2,1)S(1)} %fusion.114), channel_id=1, replica_groups=mesh['seq'=8,'head'=4] {'head'}, dimensions={1}, use_global_device_ids=true | all-gather | bytes 983040 | tf_op jit(solution)/shard_map/all_gather | solution.py:164
  237.0 5.8 convert_reduce_fusion.7
  243.7 1.7 convolution_convert_fusion
  246.1 34.5 %all-reduce.8.cloned.1.call-done = bf16[512,768]{0,1:T(8,128)(2,1)} async-done(((bf16[512,768]{0,1:T(8,128)(2,1)}), bf16[512,768]{0,1:T(8,128)(2,1)}) %all-reduce.8.cloned.1.call-update) | async-done | bytes 786448 | tf_op jit(solution)/shard_map/psum | solution.py:187
  280.6 2.4 convert_reduce_fusion.3
  283.1 1.5 fusion.102
  284.6 1.6 convert_reduce_fusion.8
  287.5 1.6 multiply_reduce_fusion
  289.1 6.5 all-reduce.2
  298.0 104.5 %while.43 = (s32[]{:T(128)}, f32[3,512,64]{1,2,0:T(8,128)S(1)}, f32[2,2048,384]{2,1,0:T(8,128)}, s32[512]{0:T(512)S(1)}, s32[2]{0:T(128)}, /*index=5*/s32[6,1]{0...) while((s32[]{:T(128)}, f32[3,512,64]{1,2,0:T(8,128)S(1)}, ...), condition=%wide.region_30.31_spmd.clone.clone.clone, body=%wide.region_27.30_spmd.clone.clone.clone.sunk | while | flops 2108366976 | bytes 175255120 | solution.py:274
  304.1 4.1 compare_and_fusion.13
  309.0 12.4 %fusion.216 = f32[3,512,2048]{1,2,0:T(8,128)S(1)} fusion(f32[3,512]{1,0:T(4,128)S(1)} %copy-done.86, f32[512,2048]{0,1:T(8,128)S(1)} %get-tuple-element.1766, pred[3,2048]{1,0:T(4,128)(4,1)S(1)} %broadcast_compare_fusion.46, pred[3,512]{1,0:T(4,128)(4,1)S(1)} %broadcast_compare_fusion.47, pred[512,2048]{0,1:T(8,128)(4,1)S(1)} %get-tuple-element.1771, ...), kind=kOutput, calls=%fused_computation.139.clone.1 | convolution fusion | flops 468713472 | bytes 22003716 | tf_op jit(solution)/shard_map/while/body/eval_jaxpr/hqd,khd->hqk/dot_general | solution.py:227
  321.4 5.1 fusion.217
  327.9 4.4 convolution_add_fusion.5
  332.3 6.7 fusion.218
  339.1 2.0 convolution_multiply_fusion.2
  341.1 1.9 maximum_bitcast_fusion.2
  343.0 3.5 copy.112
  346.5 3.7 constant_dynamic-update-slice_fusion.2
  356.4 4.1 compare_and_fusion.13
  361.2 12.4 %fusion.216 = f32[3,512,2048]{1,2,0:T(8,128)S(1)} fusion(f32[3,512]{1,0:T(4,128)S(1)} %copy-done.86, f32[512,2048]{0,1:T(8,128)S(1)} %get-tuple-element.1766, pred[3,2048]{1,0:T(4,128)(4,1)S(1)} %broadcast_compare_fusion.46, pred[3,512]{1,0:T(4,128)(4,1)S(1)} %broadcast_compare_fusion.47, pred[512,2048]{0,1:T(8,128)(4,1)S(1)} %get-tuple-element.1771, ...), kind=kOutput, calls=%fused_computation.139.clone.1 | convolution fusion | flops 468713472 | bytes 22003716 | tf_op jit(solution)/shard_map/while/body/eval_jaxpr/hqd,khd->hqk/dot_general | solution.py:227
  373.7 5.1 fusion.217
  380.1 4.4 convolution_add_fusion.5
  384.5 6.7 fusion.218
  391.3 2.0 convolution_multiply_fusion.2
  393.3 1.9 maximum_bitcast_fusion.2
  395.2 3.5 copy.112
  398.7 3.8 constant_dynamic-update-slice_fusion.2
  402.8 2.1 multiply_convert_fusion
  404.8 1.7 convolution_convert_fusion.1
  406.6 2.2 fusion.144
  408.9 2.3 fusion.131
  413.6 2.5 fusion.142
  417.4 103.4 %reduce-scatter.8.cloned.1.call-done = f32[512,384]{1,0:T(8,128)} async-done(((f32[4096,384]{1,0:T(8,128)}), f32[512,384]{1,0:T(8,128)}) %reduce-scatter.8.cloned.1.call-update) | async-done | bytes 786448 | tf_op jit(solution)/shard_map/reduce_scatter | solution.py:276
  522.1 1.5 fusion.117
  525.1 2.3 fusion.115
  531.6 14.2 %reduce-scatter.6.cloned.1.call-done = bf16[512,192]{0,1:T(8,128)(2,1)} async-done(((bf16[512,768]{0,1:T(8,128)(2,1)}), bf16[512,192]{0,1:T(8,128)(2,1)}) %reduce-scatter.6.cloned.1.call-update) | async-done | bytes 196624 | tf_op jit(solution)/shard_map/reduce_scatter | solution.py:170
  545.7 2.0 add_convert_fusion.2
  547.7 1.7 convert_reduce_fusion.9
  549.4 33.4 %all-reduce.10.cloned.1.call-done = bf16[512,768]{0,1:T(8,128)(2,1)} async-done(((bf16[512,768]{0,1:T(8,128)(2,1)}), bf16[512,768]{0,1:T(8,128)(2,1)}) %all-reduce.10.cloned.1.call-update) | async-done | bytes 786448 | tf_op jit(solution)/shard_map/psum | solution.py:291
  582.8 2.5 fusion.103
  585.3 40.1 %all-reduce = (f32[768]{0:T(1024)}, f32[768]{0:T(1024)}, f32[192]{0:T(256)}, f32[192]{0:T(256)}, f32[192]{0:T(256)}, /*index=5*/f32[192]{0:T(256)}, f32[768]{0:T...) all-reduce(f32[768]{0:T(1024)} %get-tuple-element.1251, ...), channel_id=1, replica_groups=mesh['seq'=8,'head'=4] {'seq'}, use_global_device_ids=true, to_apply=%region_36.37 | all-reduce | flops 6144 | bytes 49152 | tf_op jit(solution)/shard_map/psum | solution.py:296
  626.1 1.6 fusion.138
  628.6 198.8 %all-reduce.12.cloned.1.call-done = (f32[768,192]{0,1:T(8,128)}, f32[768,192]{0,1:T(8,128)}, f32[768,192]{0,1:T(8,128)}, f32[192,768]{1,0:T(8,128)}, f32[768,768]{1,0:T(8,128)}, /*index=5*/f32[768,768]{1,0:T(8,128)}) async-done(((f32[768,192]{0,1:T(8,128)}, f32[768,192]{0,1:T(8,128)}, f32[768,192]{0,1:T(8,128)}, f32[192,768]{1,0:T(8,128)}, f32[768,768]{1,0:T(8,128)}, /*index=5*/f32[768,768]{1,0:T(8,128)}), ...) | async-done | bytes 7077904 | tf_op jit(solution)/shard_map/psum | solution.py:296
  827.4 2.0 copy.143
  831.9 1.4 copy.147
  834.4 1.4 copy.148
  (413 shorter events, 59.7 us)
Async XLA Ops:
  7.2 229.8 %copy-start = (bf16[768,768]{1,0:T(8,128)(2,1)S(1)}, bf16[768,768]{1,0:T(8,128)(2,1)}, u32[]{:S(2)}) copy-start(bf16[768,768]{1,0:T(8,128)(2,1)} %param.40) | copy-start | bytes 3538948
  7.2 11.5 %copy-start.87 = (f32[768]{0:T(1024)S(1)}, f32[768]{0:T(1024)}, u32[]{:S(2)}) copy-start(f32[768]{0:T(1024)} %param.26) | copy-start | bytes 9220
  7.2 11.5 %copy-start.70 = (f32[768]{0:T(1024)S(1)}, f32[768]{0:T(1024)}, u32[]{:S(2)}) copy-start(f32[768]{0:T(1024)} %param.25) | copy-start | bytes 9220
  7.2 59.4 %all-gather.3.cloned.1.call-start = ((), (), s32[]{:S(2)}) async-start(), calls=%async_computation.3 | async-start | bytes 1769472 | tf_op jit(solution)/shard_map/all_gather | solution.py:136
  20.3 92.5 %all-gather.5.cloned.1.call-start = ((), (), s32[]{:S(2)}) async-start(), calls=%async_computation.4 | async-start | bytes 1769472 | tf_op jit(solution)/shard_map/all_gather | solution.py:137
  21.4 204.1 %reduce-scatter.4.cloned.1.call-start = ((), (), s32[]{:S(2)}) async-start(), calls=%async_computation.5 | async-start | bytes 983040 | tf_op jit(solution)/shard_map/reduce_scatter | solution.py:156
  124.5 12.8 %copy-start.2 = (f32[512,2048]{0,1:T(8,128)}, f32[512,2048]{0,1:T(8,128)S(1)}, u32[]{:S(2)}) copy-start(f32[512,2048]{0,1:T(8,128)S(1)} %get-tuple-element.1711) | copy-start | bytes 12582916 | tf_op jit(solution)/shard_map/while
  124.5 12.8 %copy-start.3 = (pred[512,2048]{0,1:T(8,128)(4,1)}, pred[512,2048]{0,1:T(8,128)(4,1)S(1)}, u32[]{:S(2)}) copy-start(pred[512,2048]{0,1:T(8,128)(4,1)S(1)} %get-tuple-element.1720) | copy-start | bytes 3145732 | tf_op jit(solution)/shard_map/while
  124.5 12.8 %copy-start.4 = (pred[512,2048]{0,1:T(8,128)(4,1)}, pred[512,2048]{0,1:T(8,128)(4,1)S(1)}, u32[]{:S(2)}) copy-start(pred[512,2048]{0,1:T(8,128)(4,1)S(1)} %get-tuple-element.1716) | copy-start | bytes 3145732 | tf_op jit(solution)/shard_map/while
  125.1 12.3 %copy-start.55 = (pred[3,512]{1,0:T(4,128)(4,1)}, pred[3,512]{1,0:T(4,128)(4,1)S(1)}, u32[]{:S(2)}) copy-start(pred[3,512]{1,0:T(4,128)(4,1)S(1)} %broadcast_compare_fusion.43) | copy-start | bytes 4612 | tf_op jit(solution)/shard_map/while
  125.2 12.1 %copy-start.56 = (pred[3,512]{1,0:T(4,128)(4,1)}, pred[3,512]{1,0:T(4,128)(4,1)S(1)}, u32[]{:S(2)}) copy-start(pred[3,512]{1,0:T(4,128)(4,1)S(1)} %broadcast_compare_fusion.45) | copy-start | bytes 4612 | tf_op jit(solution)/shard_map/while
  137.4 16.7 %copy-start.43 = (f32[3,512]{1,0:T(4,128)S(1)}, f32[3,512]{1,0:T(4,128)}, u32[]{:S(2)}) copy-start(f32[3,512]{1,0:T(4,128)} %get-tuple-element.1804) | copy-start | bytes 18436 | tf_op jit(solution)/shard_map/while
  137.4 16.8 %copy-start.5 = (bf16[2,2048,3,64]{1,3,2,0:T(8,128)(2,1)S(1)}, bf16[2,2048,3,64]{1,3,2,0:T(8,128)(2,1)}, u32[]{:S(2)}) copy-start(bf16[2,2048,3,64]{1,3,2,0:T(8,128)(2,1)} %get-tuple-element.1834) | copy-start | bytes 4718596 | tf_op jit(solution)/shard_map/while
  137.4 16.8 %copy-start.17 = (f32[3,512,64]{1,2,0:T(8,128)S(1)}, f32[3,512,64]{1,2,0:T(8,128)}, u32[]{:S(2)}) copy-start(f32[3,512,64]{1,2,0:T(8,128)} %get-tuple-element.1805) | copy-start | bytes 1179652 | tf_op jit(solution)/shard_map/while
  163.4 12.8 %copy-start.2 = (f32[512,2048]{0,1:T(8,128)}, f32[512,2048]{0,1:T(8,128)S(1)}, u32[]{:S(2)}) copy-start(f32[512,2048]{0,1:T(8,128)S(1)} %get-tuple-element.1711) | copy-start | bytes 12582916 | tf_op jit(solution)/shard_map/while
  163.4 12.8 %copy-start.3 = (pred[512,2048]{0,1:T(8,128)(4,1)}, pred[512,2048]{0,1:T(8,128)(4,1)S(1)}, u32[]{:S(2)}) copy-start(pred[512,2048]{0,1:T(8,128)(4,1)S(1)} %get-tuple-element.1720) | copy-start | bytes 3145732 | tf_op jit(solution)/shard_map/while
  163.4 12.8 %copy-start.4 = (pred[512,2048]{0,1:T(8,128)(4,1)}, pred[512,2048]{0,1:T(8,128)(4,1)S(1)}, u32[]{:S(2)}) copy-start(pred[512,2048]{0,1:T(8,128)(4,1)S(1)} %get-tuple-element.1716) | copy-start | bytes 3145732 | tf_op jit(solution)/shard_map/while
  164.0 12.3 %copy-start.55 = (pred[3,512]{1,0:T(4,128)(4,1)}, pred[3,512]{1,0:T(4,128)(4,1)S(1)}, u32[]{:S(2)}) copy-start(pred[3,512]{1,0:T(4,128)(4,1)S(1)} %broadcast_compare_fusion.43) | copy-start | bytes 4612 | tf_op jit(solution)/shard_map/while
  164.1 12.1 %copy-start.56 = (pred[3,512]{1,0:T(4,128)(4,1)}, pred[3,512]{1,0:T(4,128)(4,1)S(1)}, u32[]{:S(2)}) copy-start(pred[3,512]{1,0:T(4,128)(4,1)S(1)} %broadcast_compare_fusion.45) | copy-start | bytes 4612 | tf_op jit(solution)/shard_map/while
  176.3 16.7 %copy-start.43 = (f32[3,512]{1,0:T(4,128)S(1)}, f32[3,512]{1,0:T(4,128)}, u32[]{:S(2)}) copy-start(f32[3,512]{1,0:T(4,128)} %get-tuple-element.1804) | copy-start | bytes 18436 | tf_op jit(solution)/shard_map/while
  176.3 16.8 %copy-start.5 = (bf16[2,2048,3,64]{1,3,2,0:T(8,128)(2,1)S(1)}, bf16[2,2048,3,64]{1,3,2,0:T(8,128)(2,1)}, u32[]{:S(2)}) copy-start(bf16[2,2048,3,64]{1,3,2,0:T(8,128)(2,1)} %get-tuple-element.1834) | copy-start | bytes 4718596 | tf_op jit(solution)/shard_map/while
  176.3 16.8 %copy-start.17 = (f32[3,512,64]{1,2,0:T(8,128)S(1)}, f32[3,512,64]{1,2,0:T(8,128)}, u32[]{:S(2)}) copy-start(f32[3,512,64]{1,2,0:T(8,128)} %get-tuple-element.1805) | copy-start | bytes 1179652 | tf_op jit(solution)/shard_map/while
  195.1 7.3 copy-start.48
  195.1 7.3 copy-start.51
  195.2 7.3 copy-start.54
  195.2 8.8 %copy-start.59 = (s32[6,1]{0,1:T(1,128)}, s32[6,1]{0,1:T(1,128)S(1)}, u32[]{:S(2)}) copy-start(s32[6,1]{0,1:T(1,128)S(1)} %get-tuple-element.1979) | copy-start | bytes 76
  195.2 8.8 %copy-start.62 = (s32[1,6]{1,0:T(1,128)}, s32[1,6]{1,0:T(1,128)S(1)}, u32[]{:S(2)}) copy-start(s32[1,6]{1,0:T(1,128)S(1)} %get-tuple-element.1980) | copy-start | bytes 76
  195.2 7.4 copy-start.37
  195.2 7.4 copy-start.82
  195.2 7.4 copy-start.88
  196.3 7.7 copy-start.19
  202.5 11.1 %copy-start.76 = (f32[512]{0:T(512)}, f32[512]{0:T(512)S(1)}, u32[]{:S(2)}) copy-start(f32[512]{0:T(512)S(1)} %get-tuple-element.1435) | copy-start | bytes 6148
  202.5 11.1 %copy-start.78 = (f32[512]{0:T(512)}, f32[512]{0:T(512)S(1)}, u32[]{:S(2)}) copy-start(f32[512]{0:T(512)S(1)} %get-tuple-element.1436) | copy-start | bytes 6148
  202.6 10.9 %copy-start.27 = (f32[512,192]{0,1:T(8,128)}, f32[512,192]{0,1:T(8,128)S(1)}, u32[]{:S(2)}) copy-start(f32[512,192]{0,1:T(8,128)S(1)} %fusion.112) | copy-start | bytes 1179652
  202.6 22.9 %copy-start.32 = (bf16[512,192]{0,1:T(8,128)(2,1)S(1)}, bf16[512,192]{0,1:T(8,128)(2,1)}, u32[]{:S(2)}) copy-start(bf16[512,192]{0,1:T(8,128)(2,1)} %param.24) | copy-start | bytes 589828
  204.0 76.6 %all-reduce.8.cloned.1.call-start = ((), (), s32[]{:S(2)}) async-start(), calls=%async_computation.7 | async-start | bytes 1572864 | tf_op jit(solution)/shard_map/psum | solution.py:187
  204.9 30.6 %copy-start.85 = (f32[192]{0:T(256)}, f32[192]{0:T(256)S(1)}, u32[]{:S(2)}) copy-start(f32[192]{0:T(256)S(1)} %dynamic_slice.65) | copy-start | bytes 2308
  213.5 23.4 %copy-start.23 = (bf16[512,768]{0,1:T(8,128)(2,1)}, bf16[512,768]{0,1:T(8,128)(2,1)S(1)}, u32[]{:S(2)}) copy-start(bf16[512,768]{0,1:T(8,128)(2,1)S(1)} %all_gather.21) | copy-start | bytes 2359300
  213.5 22.2 %copy-start.67 = (f32[768]{0:T(1024)S(1)}, f32[768]{0:T(1024)}, u32[]{:S(2)}) copy-start(f32[768]{0:T(1024)} %param.36) | copy-start | bytes 9220
  213.6 22.2 %copy-start.93 = (f32[768]{0:T(1024)S(1)}, f32[768]{0:T(1024)}, u32[]{:S(2)}) copy-start(f32[768]{0:T(1024)} %param.39) | copy-start | bytes 9220
  213.6 22.2 %copy-start.94 = (f32[768]{0:T(1024)S(1)}, f32[768]{0:T(1024)}, u32[]{:S(2)}) copy-start(f32[768]{0:T(1024)} %param.37) | copy-start | bytes 9220
  225.5 10.3 %copy-start.92 = (bf16[768,768]{1,0:T(8,128)(2,1)S(1)}, bf16[768,768]{1,0:T(8,128)(2,1)}, u32[]{:S(2)}) copy-start(bf16[768,768]{1,0:T(8,128)(2,1)} %param.38) | copy-start | bytes 3538948
  235.3 49.3 %copy-start.9 = (bf16[512,768]{0,1:T(8,128)(2,1)}, bf16[512,768]{0,1:T(8,128)(2,1)S(1)}, u32[]{:S(2)}) copy-start(bf16[512,768]{0,1:T(8,128)(2,1)S(1)} %all_gather.20) | copy-start | bytes 2359300
  235.5 49.1 %copy-start.65 = (f32[512]{0:T(512)}, f32[512]{0:T(512)S(1)}, u32[]{:S(2)}) copy-start(f32[512]{0:T(512)S(1)} %broadcast_multiply_fusion.1) | copy-start | bytes 6148
  235.8 48.8 %copy-start.74 = (f32[512]{0:T(512)}, f32[512]{0:T(512)S(1)}, u32[]{:S(2)}) copy-start(f32[512]{0:T(512)S(1)} %fusion.123) | copy-start | bytes 6148
  243.7 36.9 %copy-start.68 = (f32[768]{0:T(1024)S(1)}, f32[768]{0:T(1024)}, u32[]{:S(2)}) copy-start(f32[768]{0:T(1024)} %param.36) | copy-start | bytes 9220
  245.5 275.3 %reduce-scatter.8.cloned.1.call-start = ((), (), s32[]{:S(2)}) async-start(), calls=%async_computation.8 | async-start | bytes 7077888 | tf_op jit(solution)/shard_map/reduce_scatter | solution.py:276
  286.3 9.4 %copy-start.77 = (f32[512]{0:T(512)S(1)}, f32[512]{0:T(512)}, u32[]{:S(2)}) copy-start(f32[512]{0:T(512)} %copy-done.76) | copy-start | bytes 6148
  286.3 9.4 %copy-start.79 = (f32[512]{0:T(512)S(1)}, f32[512]{0:T(512)}, u32[]{:S(2)}) copy-start(f32[512]{0:T(512)} %copy-done.78) | copy-start | bytes 6148
  287.5 10.5 %copy-start.6 = (bf16[2,2048,3,64]{1,3,2,0:T(8,128)(2,1)S(1)}, bf16[2,2048,3,64]{1,3,2,0:T(8,128)(2,1)}, u32[]{:S(2)}) copy-start(bf16[2,2048,3,64]{1,3,2,0:T(8,128)(2,1)} %get-tuple-element.1936) | copy-start | bytes 4718596
  321.4 6.4 copy-start.1
  327.9 11.2 %slice-start = ((s8[6291456]{0:T(1024)(128)(4,1)}), s8[4194304]{0:T(1024)(128)(4,1)S(1)}, s32[]{:S(2)}) async-start(s8[6291456]{0:T(1024)(128)(4,1)} %bitcast.169), calls=%async_computation.11 | async-start | bytes 8388608 | tf_op jit(solution)/shard_map/while
  332.3 6.8 slice-start.1
  373.6 6.4 copy-start.1
  380.1 11.2 %slice-start = ((s8[6291456]{0:T(1024)(128)(4,1)}), s8[4194304]{0:T(1024)(128)(4,1)S(1)}, s32[]{:S(2)}) async-start(s8[6291456]{0:T(1024)(128)(4,1)} %bitcast.169), calls=%async_computation.11 | async-start | bytes 8388608 | tf_op jit(solution)/shard_map/while
  384.5 6.8 slice-start.1
  402.5 143.2 %reduce-scatter.6.cloned.1.call-start = ((), (), s32[]{:S(2)}) async-start(), calls=%async_computation.6 | async-start | bytes 983040 | tf_op jit(solution)/shard_map/reduce_scatter | solution.py:170
  411.2 171.6 %all-reduce.10.cloned.1.call-start = ((), (), s32[]{:S(2)}) async-start(), calls=%async_computation.9 | async-start | bytes 1572864 | tf_op jit(solution)/shard_map/psum | solution.py:291
  525.1 302.3 %all-reduce.12.cloned.1.call-start = ((), (), s32[]{:S(2)}) async-start(), calls=%async_computation.10 | async-start | bytes 14155776 | tf_op jit(solution)/shard_map/psum | solution.py:296
  528.8 54.0 %copy-start.64 = (f32[512]{0:T(512)S(1)}, f32[512]{0:T(512)}, u32[]{:S(2)}) copy-start(f32[512]{0:T(512)} %copy-done.63) | copy-start | bytes 6148
  528.8 54.0 %copy-start.71 = (f32[768]{0:T(1024)S(1)}, f32[768]{0:T(1024)}, u32[]{:S(2)}) copy-start(f32[768]{0:T(1024)} %param.25) | copy-start | bytes 9220
  528.8 54.0 %copy-start.73 = (f32[512]{0:T(512)S(1)}, f32[512]{0:T(512)}, u32[]{:S(2)}) copy-start(f32[512]{0:T(512)} %copy-done.72) | copy-start | bytes 6148
  528.8 54.0 %copy-start.12 = (bf16[512,768]{0,1:T(8,128)(2,1)S(1)}, bf16[512,768]{0,1:T(8,128)(2,1)}, u32[]{:S(2)}) copy-start(bf16[512,768]{0,1:T(8,128)(2,1)} %copy-done.11) | copy-start | bytes 2359300
  528.8 96.6 %copy-start.81 = (f32[512]{0:T(512)S(1)}, f32[512]{0:T(512)}, u32[]{:S(2)}) copy-start(f32[512]{0:T(512)} %copy-done.80) | copy-start | bytes 6148
  (71 other events, 182.1 us)
Sparse Core Ops, SparseCore 0:
  20.4 46.1 all-gather.2
  69.2 43.4 all-gather.4
  204.2 21.3 reduce-scatter.3
  245.6 34.9 all-reduce.7
  402.6 118.0 reduce-scatter.7
  523.3 22.3 reduce-scatter.5
  548.1 34.6 all-reduce.9
  589.6 237.7 all-reduce.11
where the time goes:
time: 852 us; the launch traced here: 843 us
  waiting for transfers between devices  482 us (57%)
  matrix products  120 us (14%)
  other arithmetic  95.7 us (11%)
  blocking collectives  80.4 us (9%)
  local copies, waits for them, and re-layouts  48.5 us (6%)
  between operations  15.1 us (2%)
    psum x1, waiting for transfers between devices, shards(): lax.psum((grad_ln1_gain, grad_ln1_bias, grad_w_query, grad_b_query, grad_...  199 us
    reduce_scatter x1, waiting for transfers between devices, shards(): lax.psum_scatter(key_terms, 'seq', scatter_dimension=0, tiled=True)  103 us
    all_gather x1, waiting for transfers between devices, shards(): lax.all_gather(key_rows, 'seq', axis=0, tiled=True)  43.9 us
    all_gather x1, waiting for transfers between devices, shards(): lax.all_gather(values, 'seq', axis=0, tiled=True)  41.5 us
    psum x1, blocking collectives, shards(): lax.psum((grad_ln1_gain, grad_ln1_bias, grad_w_query, grad_b_query, grad_...  40.1 us
    psum x1, waiting for transfers between devices, shards(): lax.psum(jnp.dot(grad_inner, w_up.T, preferred_element_type=jnp.float32)....  34.5 us
    psum x1, waiting for transfers between devices, shards(): lax.psum(grad_normed.astype(jnp.bfloat16), 'head').astype(jnp.float32)  33.4 us
    reduce_sum x2, other arithmetic, advance(): totals = totals * factor + jnp.sum(weights, axis=-1)  33.3 us
  transfers between devices with their start and end apart: 8, of which 8 were waited for; matrix products, arithmetic and copies ran while one was open for 5% of the time, Pallas kernels for 0%

commit v1 on v0

--- a/solution.py
+++ b/solution.py
@@ -9,6 +9,22 @@
 eps = 1e-05
 segment_scales = (1, 2, 4, 8, 16)
 dilation_steps = (1, 2, 4, 6, 12)
+
+
+def ring_gather(x, axis, dim):
+    ways, here, hop = (lax.axis_size(axis), lax.axis_index(axis), x.shape[dim])
+    shape = [n * ways if d == dim else n for d, n in enumerate(x.shape)]
+    full = lax.dynamic_update_slice_in_dim(jnp.zeros(shape, x.dtype), x, here * hop, axis=dim)
+    going_up = going_down = x
+    for far in range(1, ways // 2 + 1):
+        going_up = lax.ppermute(going_up, axis, [(d, (d + 1) % ways) for d in range(ways)])
+        full = lax.dynamic_update_slice_in_dim(full, going_up, (here - far) % ways * hop, axis=dim)
+        if 2 * far < ways:
+            going_down = lax.ppermute(going_down, axis, [(d, (d - 1) % ways) for d in range(ways)])
+            full = lax.dynamic_update_slice_in_dim(
+                full, going_down, (here + far) % ways * hop, axis=dim
+            )
+    return full
 
 
 def layer_norm(inputs, norm_gain, norm_bias):
@@ -132,10 +148,7 @@
     )
     highest, totals, running_sum = fold_keys(
         start_state,
-        (
-            lax.all_gather(key_rows, "seq", axis=0, tiled=True),
-            lax.all_gather(values, "seq", axis=0, tiled=True),
-        ),
+        (lax.all_gather(key_rows, "seq", axis=0, tiled=True), ring_gather(values, "seq", 0)),
         query_heads,
         head_ids,
         query_row,

time: 852 us -> 844 us (level)
  waiting for transfers between devices: 482 us -> 445 us
  starting transfers between devices: 0.54 us -> 18 us
  local copies, waits for them, and re-layouts: 48.5 us -> 60.5 us
    all_gather x1, waiting for transfers between devices: 43.9 us -> 0.83 us  [shards(): lax.all_gather(key_rows, 'seq', axis=0, tiled=True)]
    ppermute x0 -> x7, waiting for transfers between devices: none -> 25.2 us  [the longest x4 25.2 us: ring_gather(): lax.ppermute(going_up, axis, [(d, (d + 1) % ways) for d in range(ways)])]
    ppermute x0 -> x7, starting transfers between devices: none -> 17.4 us  [the longest x3 9.17 us: ring_gather(): lax.ppermute(going_down, axis, [(d, (d - 1) % ways) for d in range(ways)])]
    all_gather x1, waiting for transfers between devices: 41.5 us -> 28.7 us  [shards(): lax.all_gather(values, 'seq', axis=0, tiled=True)]
    unnamed x158 -> x163, local copies, waits for them, and re-layouts: 15.4 us -> 18.8 us
  transfers between devices with their start and end apart: 8 -> 15, of which waited for: 8 -> 12; matrix products, arithmetic and copies ran while one was open for 5% -> 8% of each run, Pallas kernels for 0% -> 0%
where the time goes in v1:
time: 844 us; the launch traced here: 834 us
  waiting for transfers between devices  445 us (53%)
  matrix products  120 us (14%)
  other arithmetic  95.3 us (11%)
  blocking collectives  80 us (9%)
  local copies, waits for them, and re-layouts  60.5 us (7%)
  starting transfers between devices  18 us (2%)
  between operations  15.1 us (2%)
    psum x1, waiting for transfers between devices, shards(): lax.psum((grad_ln1_gain, grad_ln1_bias, grad_w_query, grad_b_query, grad_...  199 us
    reduce_scatter x1, waiting for transfers between devices, shards(): lax.psum_scatter(key_terms, 'seq', scatter_dimension=0, tiled=True)  103 us
    psum x1, blocking collectives, shards(): lax.psum((grad_ln1_gain, grad_ln1_bias, grad_w_query, grad_b_query, grad_...  40.1 us
    psum x1, waiting for transfers between devices, shards(): lax.psum(grad_normed.astype(jnp.bfloat16), 'head').astype(jnp.float32)  33.3 us
    reduce_sum x2, other arithmetic, advance(): totals = totals * factor + jnp.sum(weights, axis=-1)  33.3 us
    all_gather x1, waiting for transfers between devices, shards(): lax.all_gather(values, 'seq', axis=0, tiled=True)  28.7 us
    psum x1, waiting for transfers between devices, shards(): lax.psum(jnp.dot(grad_inner, w_up.T, preferred_element_type=jnp.float32)....  27.4 us
    ppermute x4, waiting for transfers between devices, ring_gather(): lax.ppermute(going_up, axis, [(d, (d + 1) % ways) for d in range(ways)])  25.2 us
  transfers between devices with their start and end apart: 15, of which 12 were waited for; matrix products, arithmetic and copies ran while one was open for 8% of the time, Pallas kernels for 0%

profile of v1, /device:TPU:0, one launch (start us, length us, event | category | flops | bytes accessed | tf_op | source)
XLA Modules:
  0.0 834.3 jit_solution(186150525657373623)
XLA Ops:
  7.3 10.4 %all_gather.16 = bf16[512,768]{0,1:T(8,128)(2,1)S(1)} all-gather(bf16[512,192]{0,1:T(8,128)(2,1)} %param.24), channel_id=1, replica_groups=mesh['seq'=8,'head'=4] {'head'}, dimensions={1}, use_global_device_ids=true | all-gather | bytes 983040 | tf_op jit(solution)/shard_map/all_gather | solution.py:134
  24.3 3.2 collective-permute-start.1
  28.2 7.0 collective-permute-done
  35.3 2.5 collective-permute-start.2
  37.7 2.8 collective-permute-start.3
  41.9 4.5 collective-permute-done.2
  46.4 1.8 collective-permute-start.4
  48.2 3.2 collective-permute-start.5
  52.8 7.7 collective-permute-done.4
  60.5 2.5 collective-permute-start.6
  64.3 6.0 collective-permute-done.6
  71.0 2.9 reshape.2802
  73.9 1.8 copy.68
  76.5 2.9 reshape.2800
  81.1 76.5 %while.42 = (s32[]{:T(128)}, f32[3,512]{1,0:T(4,128)S(1)}, f32[3,512]{1,0:T(4,128)}, f32[3,512,64]{1,2,0:T(8,128)}, s32[512]{0:T(512)S(1)}, /*index=5*/s32[2]{0:...) while((s32[]{:T(128)}, f32[3,512]{1,0:T(4,128)S(1)}, ...), condition=%wide.region_10.11_spmd.clone.clone.clone, body=%wide.region_5.10_spmd.clone.clone.clone.sunk | while | flops 955956864 | bytes 106965504 | solution.py:97
  83.4 4.1 compare_and_fusion.12
  88.3 12.1 %fusion.202 = (f32[3,512]{1,0:T(4,128)S(1)}, f32[3,2048,512]{2,1,0:T(8,128)}) fusion(f32[512,2048]{0,1:T(8,128)S(1)} %get-tuple-element.1713, pred[3,2048]{1,0:T(4,128)(4,1)S(1)} %broadcast_compare_fusion.38, pred[3,512]{1,0:T(4,128)(4,1)S(1)} %broadcast_compare_fusion.39, pred[512,2048]{0,1:T(8,128)(4,1)S(1)} %get-tuple-element.1718, ...), kind=kOutput, calls=%fused_computation.7.clone.1 | convolution fusion | flops 465566208 | bytes 22001668 | tf_op jit(solution)/shard_map/while/body/eval_jaxpr/hqd,khd->hqk/dot_general | solution.py:81
  100.5 16.7 %fusion.203 = (f32[3,512]{1,0:T(4,128)S(1)}, bf16[3,512,2048]{1,2,0:T(8,128)(2,1)S(1)}) fusion(f32[3,512]{1,0:T(4,128)S(1)} %select_maximum_fusion.2, f32[3,2048,512]{2,1,0:T(8,128)} %get-tuple-element.1732, pred[3,2048]{1,0:T(4,128)(4,1)S(1)} %broadcast_compare_fusion.38, pred[3,512]{1,0:T(4,128)(4,1)S(1)} %broadcast_compare_fusion.39, ...), kind=kLoop, calls=%fused_computation.396.clone.1 | loop fusion | flops 72350208 | bytes 27305984 | tf_op jit(solution)/shard_map/while/body/eval_jaxpr/reduce_sum | solution.py:88
  121.7 4.1 compare_and_fusion.12
  126.6 12.1 %fusion.202 = (f32[3,512]{1,0:T(4,128)S(1)}, f32[3,2048,512]{2,1,0:T(8,128)}) fusion(f32[512,2048]{0,1:T(8,128)S(1)} %get-tuple-element.1713, pred[3,2048]{1,0:T(4,128)(4,1)S(1)} %broadcast_compare_fusion.38, pred[3,512]{1,0:T(4,128)(4,1)S(1)} %broadcast_compare_fusion.39, pred[512,2048]{0,1:T(8,128)(4,1)S(1)} %get-tuple-element.1718, ...), kind=kOutput, calls=%fused_computation.7.clone.1 | convolution fusion | flops 465566208 | bytes 22001668 | tf_op jit(solution)/shard_map/while/body/eval_jaxpr/hqd,khd->hqk/dot_general | solution.py:81
  138.8 16.7 %fusion.203 = (f32[3,512]{1,0:T(4,128)S(1)}, bf16[3,512,2048]{1,2,0:T(8,128)(2,1)S(1)}) fusion(f32[3,512]{1,0:T(4,128)S(1)} %select_maximum_fusion.2, f32[3,2048,512]{2,1,0:T(8,128)} %get-tuple-element.1732, pred[3,2048]{1,0:T(4,128)(4,1)S(1)} %broadcast_compare_fusion.38, pred[3,512]{1,0:T(4,128)(4,1)S(1)} %broadcast_compare_fusion.39, ...), kind=kLoop, calls=%fused_computation.396.clone.1 | loop fusion | flops 72350208 | bytes 27305984 | tf_op jit(solution)/shard_map/while/body/eval_jaxpr/reduce_sum | solution.py:88
  158.9 6.3 all-reduce.3
  167.6 8.5 %all_gather.19 = bf16[512,768]{0,1:T(8,128)(2,1)S(1)} all-gather(bf16[512,192]{0,1:T(8,128)(2,1)} %param.42), channel_id=1, replica_groups=mesh['seq'=8,'head'=4] {'head'}, dimensions={1}, use_global_device_ids=true | all-gather | bytes 983040 | tf_op jit(solution)/shard_map/all_gather | solution.py:191
  176.9 11.9 %reduce-scatter.4.cloned.1.call-done = bf16[512,192]{0,1:T(8,128)(2,1)} async-done(((bf16[512,768]{0,1:T(8,128)(2,1)}), bf16[512,192]{0,1:T(8,128)(2,1)}) %reduce-scatter.4.cloned.1.call-update) | async-done | bytes 196624 | tf_op jit(solution)/shard_map/reduce_scatter | solution.py:169
  190.0 8.2 all_gather.18
  199.8 5.8 convert_reduce_fusion.7
  208.3 28.7 %all-gather.5.cloned.1.call-done = bf16[4096,192]{0,1:T(8,128)(2,1)} async-done(((bf16[512,192]{0,1:T(8,128)(2,1)}), bf16[4096,192]{0,1:T(8,128)(2,1)}) %all-gather.5.cloned.1.call-update) | async-done | bytes 1572880 | tf_op jit(solution)/shard_map/all_gather | solution.py:227
  237.0 3.9 reshape.2804
  240.9 3.3 copy.71
  244.8 27.4 %all-reduce.8.cloned.1.call-done = bf16[512,768]{0,1:T(8,128)(2,1)} async-done(((bf16[512,768]{0,1:T(8,128)(2,1)}), bf16[512,768]{0,1:T(8,128)(2,1)}) %all-reduce.8.cloned.1.call-update) | async-done | bytes 786448 | tf_op jit(solution)/shard_map/psum | solution.py:200
  272.2 2.4 convert_reduce_fusion.3
  280.7 6.5 all-reduce.2
  289.6 104.3 %while.43 = (s32[]{:T(128)}, f32[3,512,64]{1,2,0:T(8,128)S(1)}, f32[2,2048,384]{2,1,0:T(8,128)}, s32[512]{0:T(512)S(1)}, s32[2]{0:T(128)}, /*index=5*/s32[6,1]{0...) while((s32[]{:T(128)}, f32[3,512,64]{1,2,0:T(8,128)S(1)}, ...), condition=%wide.region_30.31_spmd.clone.clone.clone, body=%wide.region_27.30_spmd.clone.clone.clone.sunk | while | flops 2108366976 | bytes 175255120 | solution.py:287
  295.8 4.1 compare_and_fusion.13
  300.6 12.5 %fusion.216 = f32[3,512,2048]{1,2,0:T(8,128)S(1)} fusion(f32[3,512]{1,0:T(4,128)S(1)} %copy-done.87, f32[512,2048]{0,1:T(8,128)S(1)} %get-tuple-element.1768, pred[3,2048]{1,0:T(4,128)(4,1)S(1)} %broadcast_compare_fusion.46, pred[3,512]{1,0:T(4,128)(4,1)S(1)} %broadcast_compare_fusion.47, pred[512,2048]{0,1:T(8,128)(4,1)S(1)} %get-tuple-element.1773, ...), kind=kOutput, calls=%fused_computation.139.clone.1 | convolution fusion | flops 468713472 | bytes 22003716 | tf_op jit(solution)/shard_map/while/body/eval_jaxpr/hqd,khd->hqk/dot_general | solution.py:240
  313.1 5.2 fusion.217
  319.6 4.2 convolution_add_fusion.5
  323.8 6.7 fusion.218
  330.5 2.0 convolution_multiply_fusion.2
  332.6 1.9 maximum_bitcast_fusion.2
  334.5 3.5 copy.111
  338.0 3.7 constant_dynamic-update-slice_fusion.10
  347.9 4.1 compare_and_fusion.13
  352.8 12.5 %fusion.216 = f32[3,512,2048]{1,2,0:T(8,128)S(1)} fusion(f32[3,512]{1,0:T(4,128)S(1)} %copy-done.87, f32[512,2048]{0,1:T(8,128)S(1)} %get-tuple-element.1768, pred[3,2048]{1,0:T(4,128)(4,1)S(1)} %broadcast_compare_fusion.46, pred[3,512]{1,0:T(4,128)(4,1)S(1)} %broadcast_compare_fusion.47, pred[512,2048]{0,1:T(8,128)(4,1)S(1)} %get-tuple-element.1773, ...), kind=kOutput, calls=%fused_computation.139.clone.1 | convolution fusion | flops 468713472 | bytes 22003716 | tf_op jit(solution)/shard_map/while/body/eval_jaxpr/hqd,khd->hqk/dot_general | solution.py:240
  365.2 5.2 fusion.217
  371.7 4.2 convolution_add_fusion.5
  375.9 6.7 fusion.218
  382.7 2.0 convolution_multiply_fusion.2
  384.7 1.9 maximum_bitcast_fusion.2
  386.6 3.5 copy.111
  390.1 3.8 constant_dynamic-update-slice_fusion.10
  394.1 2.1 multiply_convert_fusion
  398.0 2.2 fusion.144
  400.3 2.3 fusion.131
  405.0 2.5 fusion.142
  408.8 103.4 %reduce-scatter.8.cloned.1.call-done = f32[512,384]{1,0:T(8,128)} async-done(((f32[4096,384]{1,0:T(8,128)}), f32[512,384]{1,0:T(8,128)}) %reduce-scatter.8.cloned.1.call-update) | async-done | bytes 786448 | tf_op jit(solution)/shard_map/reduce_scatter | solution.py:289
  516.6 2.3 fusion.115
  523.0 14.2 %reduce-scatter.6.cloned.1.call-done = bf16[512,192]{0,1:T(8,128)(2,1)} async-done(((bf16[512,768]{0,1:T(8,128)(2,1)}), bf16[512,192]{0,1:T(8,128)(2,1)}) %reduce-scatter.6.cloned.1.call-update) | async-done | bytes 196624 | tf_op jit(solution)/shard_map/reduce_scatter | solution.py:183
  537.2 2.0 add_convert_fusion.2
  540.9 33.3 %all-reduce.10.cloned.1.call-done = bf16[512,768]{0,1:T(8,128)(2,1)} async-done(((bf16[512,768]{0,1:T(8,128)(2,1)}), bf16[512,768]{0,1:T(8,128)(2,1)}) %all-reduce.10.cloned.1.call-update) | async-done | bytes 786448 | tf_op jit(solution)/shard_map/psum | solution.py:304
  574.2 2.5 fusion.103
  576.7 40.1 %all-reduce = (f32[768]{0:T(1024)}, f32[768]{0:T(1024)}, f32[192]{0:T(256)}, f32[192]{0:T(256)}, f32[192]{0:T(256)}, /*index=5*/f32[192]{0:T(256)}, f32[768]{0:T...) all-reduce(f32[768]{0:T(1024)} %get-tuple-element.1251, ...), channel_id=1, replica_groups=mesh['seq'=8,'head'=4] {'seq'}, use_global_device_ids=true, to_apply=%region_36.37 | all-reduce | flops 6144 | bytes 49152 | tf_op jit(solution)/shard_map/psum | solution.py:309
  620.0 198.8 %all-reduce.12.cloned.1.call-done = (f32[768,192]{0,1:T(8,128)}, f32[768,192]{0,1:T(8,128)}, f32[768,192]{0,1:T(8,128)}, f32[192,768]{1,0:T(8,128)}, f32[768,768]{1,0:T(8,128)}, /*index=5*/f32[768,768]{1,0:T(8,128)}) async-done(((f32[768,192]{0,1:T(8,128)}, f32[768,192]{0,1:T(8,128)}, f32[768,192]{0,1:T(8,128)}, f32[192,768]{1,0:T(8,128)}, f32[768,768]{1,0:T(8,128)}, /*index=5*/f32[768,768]{1,0:T(8,128)}), ...) | async-done | bytes 7077904 | tf_op jit(solution)/shard_map/psum | solution.py:309
  818.8 2.0 copy.150
  (449 shorter events, 84.9 us)
Async XLA Ops:
  7.2 192.6 %copy-start = (bf16[768,768]{1,0:T(8,128)(2,1)S(1)}, bf16[768,768]{1,0:T(8,128)(2,1)}, u32[]{:S(2)}) copy-start(bf16[768,768]{1,0:T(8,128)(2,1)} %param.40) | copy-start | bytes 3538948
  7.2 11.5 %copy-start.88 = (f32[768]{0:T(1024)S(1)}, f32[768]{0:T(1024)}, u32[]{:S(2)}) copy-start(f32[768]{0:T(1024)} %param.26) | copy-start | bytes 9220
  7.2 11.5 %copy-start.71 = (f32[768]{0:T(1024)S(1)}, f32[768]{0:T(1024)}, u32[]{:S(2)}) copy-start(f32[768]{0:T(1024)} %param.25) | copy-start | bytes 9220
  7.2 69.3 %all-gather.3.cloned.1.call-start = ((), (), s32[]{:S(2)}) async-start(), calls=%async_computation.3 | async-start | bytes 1769472 | tf_op jit(solution)/shard_map/all_gather | solution.py:151
  19.3 8.6 %copy-start.5 = (bf16[512,768]{0,1:T(8,128)(2,1)}, bf16[512,768]{0,1:T(8,128)(2,1)S(1)}, u32[]{:S(2)}) copy-start(bf16[512,768]{0,1:T(8,128)(2,1)S(1)} %fusion.96) | copy-start | bytes 2359300
  20.3 168.5 %reduce-scatter.4.cloned.1.call-start = ((), (), s32[]{:S(2)}) async-start(), calls=%async_computation.4 | async-start | bytes 983040 | tf_op jit(solution)/shard_map/reduce_scatter | solution.py:169
  22.7 40.9 %copy-start.40 = (bf16[512,192]{0,1:T(8,128)(2,1)}, bf16[512,192]{0,1:T(8,128)(2,1)S(1)}, u32[]{:S(2)}) copy-start(bf16[512,192]{0,1:T(8,128)(2,1)S(1)} %get-tuple-element.1440) | copy-start | bytes 589828
  22.7 12.5 %collective-permute-start = (bf16[512,192]{0,1:T(8,128)(2,1)S(1)}, bf16[512,192]{0,1:T(8,128)(2,1)S(1)}, u32[]{:S(2)}, u32[]{:S(2)}) collective-permute-start(bf16[512,192]{0,1:T(8,128)(2,1)S(1)} %get-tuple-element.1440), channel_id=1, source_target_pairs={{0,4},{4,8},{8,12},{12,16},{16,20},{20,24},{24,28},{28,0},{1,5},{5... | collective-permute-start | bytes 589832 | tf_op jit(solution)/shard_map/ppermute | solution.py:20
  24.3 13.5 %collective-permute-start.1 = (bf16[512,192]{0,1:T(8,128)(2,1)S(1)}, bf16[512,192]{0,1:T(8,128)(2,1)S(1)}, u32[]{:S(2)}, u32[]{:S(2)}) collective-permute-start(bf16[512,192]{0,1:T(8,128)(2,1)S(1)} %get-tuple-element.1440), channel_id=1, source_target_pairs={{0,28},{4,0},{8,4},{12,8},{16,12},{20,16},{24,20},{28,24},{1,29},{... | collective-permute-start | bytes 589832 | tf_op jit(solution)/shard_map/ppermute | solution.py:23
  35.3 11.2 %collective-permute-start.2 = (bf16[512,192]{0,1:T(8,128)(2,1)S(1)}, bf16[512,192]{0,1:T(8,128)(2,1)S(1)}, u32[]{:S(2)}, u32[]{:S(2)}) collective-permute-start(bf16[512,192]{0,1:T(8,128)(2,1)S(1)} %collective-permute-done), channel_id=1, source_target_pairs={{0,4},{4,8},{8,12},{12,16},{16,20},{20,24},{24,28},{28,0},{1,5},{5... | collective-permute-start | bytes 589832 | tf_op jit(solution)/shard_map/ppermute | solution.py:20
  37.7 10.5 %collective-permute-start.3 = (bf16[512,192]{0,1:T(8,128)(2,1)S(1)}, bf16[512,192]{0,1:T(8,128)(2,1)S(1)}, u32[]{:S(2)}, u32[]{:S(2)}) collective-permute-start(bf16[512,192]{0,1:T(8,128)(2,1)S(1)} %collective-permute-done.1), channel_id=1, source_target_pairs={{0,28},{4,0},{8,4},{12,8},{16,12},{20,16},{24,20},{28,24},{1,29},{... | collective-permute-start | bytes 589832 | tf_op jit(solution)/shard_map/ppermute | solution.py:23
  46.4 14.1 %collective-permute-start.4 = (bf16[512,192]{0,1:T(8,128)(2,1)S(1)}, bf16[512,192]{0,1:T(8,128)(2,1)S(1)}, u32[]{:S(2)}, u32[]{:S(2)}) collective-permute-start(bf16[512,192]{0,1:T(8,128)(2,1)S(1)} %collective-permute-done.2), channel_id=1, source_target_pairs={{0,4},{4,8},{8,12},{12,16},{16,20},{20,24},{24,28},{28,0},{1,5},{5... | collective-permute-start | bytes 589832 | tf_op jit(solution)/shard_map/ppermute | solution.py:20
  48.2 15.4 %collective-permute-start.5 = (bf16[512,192]{0,1:T(8,128)(2,1)S(1)}, bf16[512,192]{0,1:T(8,128)(2,1)S(1)}, u32[]{:S(2)}, u32[]{:S(2)}) collective-permute-start(bf16[512,192]{0,1:T(8,128)(2,1)S(1)} %collective-permute-done.3), channel_id=1, source_target_pairs={{0,28},{4,0},{8,4},{12,8},{16,12},{20,16},{24,20},{28,24},{1,29},{... | collective-permute-start | bytes 589832 | tf_op jit(solution)/shard_map/ppermute | solution.py:23
  60.5 9.9 %collective-permute-start.6 = (bf16[512,192]{0,1:T(8,128)(2,1)S(1)}, bf16[512,192]{0,1:T(8,128)(2,1)S(1)}, u32[]{:S(2)}, u32[]{:S(2)}) collective-permute-start(bf16[512,192]{0,1:T(8,128)(2,1)S(1)} %collective-permute-done.4), channel_id=1, source_target_pairs={{0,4},{4,8},{8,12},{12,16},{16,20},{20,24},{24,28},{28,0},{1,5},{5... | collective-permute-start | bytes 589832 | tf_op jit(solution)/shard_map/ppermute | solution.py:20
  87.6 12.8 %copy-start.2 = (f32[512,2048]{0,1:T(8,128)}, f32[512,2048]{0,1:T(8,128)S(1)}, u32[]{:S(2)}) copy-start(f32[512,2048]{0,1:T(8,128)S(1)} %get-tuple-element.1713) | copy-start | bytes 12582916 | tf_op jit(solution)/shard_map/while
  87.6 12.8 %copy-start.3 = (pred[512,2048]{0,1:T(8,128)(4,1)}, pred[512,2048]{0,1:T(8,128)(4,1)S(1)}, u32[]{:S(2)}) copy-start(pred[512,2048]{0,1:T(8,128)(4,1)S(1)} %get-tuple-element.1722) | copy-start | bytes 3145732 | tf_op jit(solution)/shard_map/while
  87.6 12.8 %copy-start.4 = (pred[512,2048]{0,1:T(8,128)(4,1)}, pred[512,2048]{0,1:T(8,128)(4,1)S(1)}, u32[]{:S(2)}) copy-start(pred[512,2048]{0,1:T(8,128)(4,1)S(1)} %get-tuple-element.1718) | copy-start | bytes 3145732 | tf_op jit(solution)/shard_map/while
  88.2 12.3 %copy-start.56 = (pred[3,512]{1,0:T(4,128)(4,1)}, pred[3,512]{1,0:T(4,128)(4,1)S(1)}, u32[]{:S(2)}) copy-start(pred[3,512]{1,0:T(4,128)(4,1)S(1)} %broadcast_compare_fusion.43) | copy-start | bytes 4612 | tf_op jit(solution)/shard_map/while
  88.3 12.1 %copy-start.57 = (pred[3,512]{1,0:T(4,128)(4,1)}, pred[3,512]{1,0:T(4,128)(4,1)S(1)}, u32[]{:S(2)}) copy-start(pred[3,512]{1,0:T(4,128)(4,1)S(1)} %broadcast_compare_fusion.45) | copy-start | bytes 4612 | tf_op jit(solution)/shard_map/while
  100.5 16.7 %copy-start.44 = (f32[3,512]{1,0:T(4,128)S(1)}, f32[3,512]{1,0:T(4,128)}, u32[]{:S(2)}) copy-start(f32[3,512]{1,0:T(4,128)} %get-tuple-element.1806) | copy-start | bytes 18436 | tf_op jit(solution)/shard_map/while
  100.5 16.8 %copy-start.13 = (bf16[2,2048,3,64]{1,3,2,0:T(8,128)(2,1)S(1)}, bf16[2,2048,3,64]{1,3,2,0:T(8,128)(2,1)}, u32[]{:S(2)}) copy-start(bf16[2,2048,3,64]{1,3,2,0:T(8,128)(2,1)} %get-tuple-element.1836) | copy-start | bytes 4718596 | tf_op jit(solution)/shard_map/while
  100.5 16.8 %copy-start.17 = (f32[3,512,64]{1,2,0:T(8,128)S(1)}, f32[3,512,64]{1,2,0:T(8,128)}, u32[]{:S(2)}) copy-start(f32[3,512,64]{1,2,0:T(8,128)} %get-tuple-element.1807) | copy-start | bytes 1179652 | tf_op jit(solution)/shard_map/while
  125.9 12.8 %copy-start.2 = (f32[512,2048]{0,1:T(8,128)}, f32[512,2048]{0,1:T(8,128)S(1)}, u32[]{:S(2)}) copy-start(f32[512,2048]{0,1:T(8,128)S(1)} %get-tuple-element.1713) | copy-start | bytes 12582916 | tf_op jit(solution)/shard_map/while
  125.9 12.8 %copy-start.3 = (pred[512,2048]{0,1:T(8,128)(4,1)}, pred[512,2048]{0,1:T(8,128)(4,1)S(1)}, u32[]{:S(2)}) copy-start(pred[512,2048]{0,1:T(8,128)(4,1)S(1)} %get-tuple-element.1722) | copy-start | bytes 3145732 | tf_op jit(solution)/shard_map/while
  125.9 12.8 %copy-start.4 = (pred[512,2048]{0,1:T(8,128)(4,1)}, pred[512,2048]{0,1:T(8,128)(4,1)S(1)}, u32[]{:S(2)}) copy-start(pred[512,2048]{0,1:T(8,128)(4,1)S(1)} %get-tuple-element.1718) | copy-start | bytes 3145732 | tf_op jit(solution)/shard_map/while
  126.4 12.3 %copy-start.56 = (pred[3,512]{1,0:T(4,128)(4,1)}, pred[3,512]{1,0:T(4,128)(4,1)S(1)}, u32[]{:S(2)}) copy-start(pred[3,512]{1,0:T(4,128)(4,1)S(1)} %broadcast_compare_fusion.43) | copy-start | bytes 4612 | tf_op jit(solution)/shard_map/while
  126.6 12.1 %copy-start.57 = (pred[3,512]{1,0:T(4,128)(4,1)}, pred[3,512]{1,0:T(4,128)(4,1)S(1)}, u32[]{:S(2)}) copy-start(pred[3,512]{1,0:T(4,128)(4,1)S(1)} %broadcast_compare_fusion.45) | copy-start | bytes 4612 | tf_op jit(solution)/shard_map/while
  138.7 16.7 %copy-start.44 = (f32[3,512]{1,0:T(4,128)S(1)}, f32[3,512]{1,0:T(4,128)}, u32[]{:S(2)}) copy-start(f32[3,512]{1,0:T(4,128)} %get-tuple-element.1806) | copy-start | bytes 18436 | tf_op jit(solution)/shard_map/while
  138.7 16.8 %copy-start.13 = (bf16[2,2048,3,64]{1,3,2,0:T(8,128)(2,1)S(1)}, bf16[2,2048,3,64]{1,3,2,0:T(8,128)(2,1)}, u32[]{:S(2)}) copy-start(bf16[2,2048,3,64]{1,3,2,0:T(8,128)(2,1)} %get-tuple-element.1836) | copy-start | bytes 4718596 | tf_op jit(solution)/shard_map/while
  138.7 16.8 %copy-start.17 = (f32[3,512,64]{1,2,0:T(8,128)S(1)}, f32[3,512,64]{1,2,0:T(8,128)}, u32[]{:S(2)}) copy-start(f32[3,512,64]{1,2,0:T(8,128)} %get-tuple-element.1807) | copy-start | bytes 1179652 | tf_op jit(solution)/shard_map/while
  157.7 9.1 %copy-start.60 = (s32[6,1]{0,1:T(1,128)}, s32[6,1]{0,1:T(1,128)S(1)}, u32[]{:S(2)}) copy-start(s32[6,1]{0,1:T(1,128)S(1)} %get-tuple-element.1994) | copy-start | bytes 76
  157.7 9.1 %copy-start.63 = (s32[1,6]{1,0:T(1,128)}, s32[1,6]{1,0:T(1,128)S(1)}, u32[]{:S(2)}) copy-start(s32[1,6]{1,0:T(1,128)S(1)} %get-tuple-element.1995) | copy-start | bytes 76
  157.7 7.7 copy-start.37
  158.8 8.0 copy-start.19
  165.4 10.7 %copy-start.27 = (f32[512,192]{0,1:T(8,128)}, f32[512,192]{0,1:T(8,128)S(1)}, u32[]{:S(2)}) copy-start(f32[512,192]{0,1:T(8,128)S(1)} %fusion.112) | copy-start | bytes 1179652
  165.4 23.4 %copy-start.32 = (bf16[512,192]{0,1:T(8,128)(2,1)S(1)}, bf16[512,192]{0,1:T(8,128)(2,1)}, u32[]{:S(2)}) copy-start(bf16[512,192]{0,1:T(8,128)(2,1)} %param.24) | copy-start | bytes 589828
  166.8 70.2 %all-gather.5.cloned.1.call-start = ((), (), s32[]{:S(2)}) async-start(), calls=%async_computation.7 | async-start | bytes 1769472 | tf_op jit(solution)/shard_map/all_gather | solution.py:227
  167.6 104.6 %all-reduce.8.cloned.1.call-start = ((), (), s32[]{:S(2)}) async-start(), calls=%async_computation.6 | async-start | bytes 1572864 | tf_op jit(solution)/shard_map/psum | solution.py:200
  176.1 23.7 %copy-start.23 = (bf16[512,768]{0,1:T(8,128)(2,1)}, bf16[512,768]{0,1:T(8,128)(2,1)S(1)}, u32[]{:S(2)}) copy-start(bf16[512,768]{0,1:T(8,128)(2,1)S(1)} %all_gather.19) | copy-start | bytes 2359300
  176.9 21.7 %copy-start.86 = (f32[192]{0:T(256)}, f32[192]{0:T(256)S(1)}, u32[]{:S(2)}) copy-start(f32[192]{0:T(256)S(1)} %dynamic_slice.65) | copy-start | bytes 2308
  176.9 21.8 %copy-start.68 = (f32[768]{0:T(1024)S(1)}, f32[768]{0:T(1024)}, u32[]{:S(2)}) copy-start(f32[768]{0:T(1024)} %param.36) | copy-start | bytes 9220
  176.9 21.8 %copy-start.94 = (f32[768]{0:T(1024)S(1)}, f32[768]{0:T(1024)}, u32[]{:S(2)}) copy-start(f32[768]{0:T(1024)} %param.39) | copy-start | bytes 9220
  176.9 21.8 %copy-start.95 = (f32[768]{0:T(1024)S(1)}, f32[768]{0:T(1024)}, u32[]{:S(2)}) copy-start(f32[768]{0:T(1024)} %param.37) | copy-start | bytes 9220
  188.8 9.8 %copy-start.93 = (bf16[768,768]{1,0:T(8,128)(2,1)S(1)}, bf16[768,768]{1,0:T(8,128)(2,1)}, u32[]{:S(2)}) copy-start(bf16[768,768]{1,0:T(8,128)(2,1)} %param.38) | copy-start | bytes 3538948
  198.2 78.0 %copy-start.7 = (bf16[512,768]{0,1:T(8,128)(2,1)}, bf16[512,768]{0,1:T(8,128)(2,1)S(1)}, u32[]{:S(2)}) copy-start(bf16[512,768]{0,1:T(8,128)(2,1)S(1)} %all_gather.18) | copy-start | bytes 2359300
  198.4 77.8 %copy-start.66 = (f32[512]{0:T(512)}, f32[512]{0:T(512)S(1)}, u32[]{:S(2)}) copy-start(f32[512]{0:T(512)S(1)} %broadcast_multiply_fusion.1) | copy-start | bytes 6148
  198.7 77.5 %copy-start.75 = (f32[512]{0:T(512)}, f32[512]{0:T(512)S(1)}, u32[]{:S(2)}) copy-start(f32[512]{0:T(512)S(1)} %fusion.123) | copy-start | bytes 6148
  208.3 303.9 %reduce-scatter.8.cloned.1.call-start = ((), (), s32[]{:S(2)}) async-start(), calls=%async_computation.8 | async-start | bytes 7077888 | tf_op jit(solution)/shard_map/reduce_scatter | solution.py:289
  240.9 31.3 %copy-start.69 = (f32[768]{0:T(1024)S(1)}, f32[768]{0:T(1024)}, u32[]{:S(2)}) copy-start(f32[768]{0:T(1024)} %param.36) | copy-start | bytes 9220
  277.8 9.4 %copy-start.78 = (f32[512]{0:T(512)S(1)}, f32[512]{0:T(512)}, u32[]{:S(2)}) copy-start(f32[512]{0:T(512)} %copy-done.77) | copy-start | bytes 6148
  277.8 9.4 %copy-start.80 = (f32[512]{0:T(512)S(1)}, f32[512]{0:T(512)}, u32[]{:S(2)}) copy-start(f32[512]{0:T(512)} %copy-done.79) | copy-start | bytes 6148
  279.0 10.6 %copy-start.12 = (bf16[2,2048,3,64]{1,3,2,0:T(8,128)(2,1)S(1)}, bf16[2,2048,3,64]{1,3,2,0:T(8,128)(2,1)}, u32[]{:S(2)}) copy-start(bf16[2,2048,3,64]{1,3,2,0:T(8,128)(2,1)} %get-tuple-element.1938) | copy-start | bytes 4718596
  300.6 12.5 %copy-start.14 = (bf16[2,2048,3,64]{1,3,2,0:T(8,128)(2,1)S(1)}, bf16[2,2048,3,64]{1,3,2,0:T(8,128)(2,1)}, u32[]{:S(2)}) copy-start(bf16[2,2048,3,64]{1,3,2,0:T(8,128)(2,1)} %get-tuple-element.1894) | copy-start | bytes 4718596 | tf_op jit(solution)/shard_map/while
  319.6 10.9 %slice-start = ((s8[6291456]{0:T(1024)(128)(4,1)}), s8[4194304]{0:T(1024)(128)(4,1)S(1)}, s32[]{:S(2)}) async-start(s8[6291456]{0:T(1024)(128)(4,1)} %bitcast.171), calls=%async_computation.11 | async-start | bytes 8388608 | tf_op jit(solution)/shard_map/while
  352.8 12.5 %copy-start.14 = (bf16[2,2048,3,64]{1,3,2,0:T(8,128)(2,1)S(1)}, bf16[2,2048,3,64]{1,3,2,0:T(8,128)(2,1)}, u32[]{:S(2)}) copy-start(bf16[2,2048,3,64]{1,3,2,0:T(8,128)(2,1)} %get-tuple-element.1894) | copy-start | bytes 4718596 | tf_op jit(solution)/shard_map/while
  371.7 10.9 %slice-start = ((s8[6291456]{0:T(1024)(128)(4,1)}), s8[4194304]{0:T(1024)(128)(4,1)S(1)}, s32[]{:S(2)}) async-start(s8[6291456]{0:T(1024)(128)(4,1)} %bitcast.171), calls=%async_computation.11 | async-start | bytes 8388608 | tf_op jit(solution)/shard_map/while
  393.9 143.3 %reduce-scatter.6.cloned.1.call-start = ((), (), s32[]{:S(2)}) async-start(), calls=%async_computation.5 | async-start | bytes 983040 | tf_op jit(solution)/shard_map/reduce_scatter | solution.py:183
  402.6 171.6 %all-reduce.10.cloned.1.call-start = ((), (), s32[]{:S(2)}) async-start(), calls=%async_computation.9 | async-start | bytes 1572864 | tf_op jit(solution)/shard_map/psum | solution.py:304
  516.5 302.2 %all-reduce.12.cloned.1.call-start = ((), (), s32[]{:S(2)}) async-start(), calls=%async_computation.10 | async-start | bytes 14155776 | tf_op jit(solution)/shard_map/psum | solution.py:309
  520.3 53.9 %copy-start.65 = (f32[512]{0:T(512)S(1)}, f32[512]{0:T(512)}, u32[]{:S(2)}) copy-start(f32[512]{0:T(512)} %copy-done.64) | copy-start | bytes 6148
  520.3 53.9 %copy-start.72 = (f32[768]{0:T(1024)S(1)}, f32[768]{0:T(1024)}, u32[]{:S(2)}) copy-start(f32[768]{0:T(1024)} %param.25) | copy-start | bytes 9220
  520.3 53.9 %copy-start.74 = (f32[512]{0:T(512)S(1)}, f32[512]{0:T(512)}, u32[]{:S(2)}) copy-start(f32[512]{0:T(512)} %copy-done.73) | copy-start | bytes 6148
  520.3 53.9 %copy-start.10 = (bf16[512,768]{0,1:T(8,128)(2,1)S(1)}, bf16[512,768]{0,1:T(8,128)(2,1)}, u32[]{:S(2)}) copy-start(bf16[512,768]{0,1:T(8,128)(2,1)} %copy-done.9) | copy-start | bytes 2359300
  520.3 96.5 %copy-start.82 = (f32[512]{0:T(512)S(1)}, f32[512]{0:T(512)}, u32[]{:S(2)}) copy-start(f32[512]{0:T(512)} %copy-done.81) | copy-start | bytes 6148
  (84 other events, 258.3 us)
Sparse Core Ops, SparseCore 0:
  20.4 55.9 all-gather.2
  166.9 21.8 reduce-scatter.3
  191.6 45.3 all-gather.4
  239.4 32.7 all-reduce.7
  394.0 118.1 reduce-scatter.7
  514.7 22.4 reduce-scatter.5
  539.6 34.5 all-reduce.9
  581.0 237.7 all-reduce.11
